TPU v7x, 256 devices: a whole 4x4x8 slice. The times are simulated.
256 devices in a mesh: grp: 64 (over y, z, core), sub: 4 (over x).
Axes of the slice: x: 4, y: 4, z: 8, core: 2. Of those that a mesh axis runs over, the one named last changes fastest.
Arguments:
- adj_next: float32 [64, 128, 128, 128], P('grp', 'sub'), may hold values from -4.5 to 4.5
- adj_later: float32 [64, 128, 128, 128], P('grp', 'sub'), may hold values from -2.25 to 2.25
- box_sizes: int32 [64, 2], replicated, may hold values from 64 to 128, as said below
- holder: int32 [64], replicated, may hold values from 0 to 63, as said below
- partner: int32 [64, 2, 4], replicated, may hold values from -1 to 255, as said below
Outputs:
- adj_now: float32 [64, 128, 128, 128], P('grp', 'sub')
- adj_earlier: float32 [64, 128, 128, 128], P('grp', 'sub')
Inputs may be any that keep to these rules, and one draw needn't show every extreme that they name: box_sizes[p] = (Lx, Ly) with 64 <= Lx <= 128 and 64 <= Ly <= 128; some partition has Lx = 128 and Ly = 128, some has Lx = 64, some has Ly = 64. holder names every slot exactly once. The joining is mutual: if partner[p, f, s] = q * 4 + t then partner[q, 1 - f, t] = p * 4 + s, and q differs from p. A face may be joined in part and walled in part; some faces are wholly walls. Over both faces, a partition has at most 3 segments joined to any one other partition, and some pair of partitions has exactly 3.
All inputs are finite; a program needn't handle non-finite values.
Results may differ from a plain program's by a relative error of at most 0.0003.
Values sent between devices are 32-bit elements; how exact they have to be, the bound alone decides.
A program may use at most 128 MiB of HBM per device.

v0:
```python
import jax
import jax.numpy as jnp
from jax import lax
from jax.sharding import PartitionSpec as P

time_step = 0.5
precise = lax.Precision.HIGHEST
stencil_rows = (
    (0, 0, -2, 2, 0, 0),
    (0, 2, -27, 27, -2, 0),
    (-2, 27, -270, 270, -27, 2),
    (2, -27, 270, -270, 27, -2),
    (0, -2, 27, -27, 2, 0),
    (0, 0, 2, -2, 0, 0),
)


def cosine_table(size_cells, length):
    mode_index = jnp.arange(size_cells, dtype=jnp.int32)[:, None]
    cell_index = jnp.arange(size_cells, dtype=jnp.int32)[None, :]
    extent = length.astype(jnp.float32)
    angles = (
        jnp.pi * mode_index.astype(jnp.float32) * (cell_index.astype(jnp.float32) + 0.5) / extent
    )
    scaling = jnp.sqrt(jnp.where(mode_index == 0, 1.0, 2.0).astype(jnp.float32) / extent)
    inside = (mode_index < length) & (cell_index < length)
    return jnp.where(inside, scaling * jnp.cos(angles), jnp.float32(0.0))


def update_factors(len_x, len_y, first_y, count_y, total_x, total_z):
    wave_x = jnp.arange(total_x, dtype=jnp.int32).astype(jnp.float32) / len_x.astype(jnp.float32)
    wave_y = (first_y + jnp.arange(count_y, dtype=jnp.int32)).astype(jnp.float32) / len_y.astype(
        jnp.float32
    )
    wave_z = jnp.arange(total_z, dtype=jnp.int32).astype(jnp.float32) / jnp.float32(total_z)
    angular = jnp.pi * jnp.sqrt(
        wave_x[:, None, None] ** 2 + wave_y[None, :, None] ** 2 + wave_z[None, None, :] ** 2
    )
    two_cos = 2.0 * jnp.cos(angular * time_step)
    source = time_step**2 * jnp.sinc(angular * (time_step / (2.0 * jnp.pi))) ** 2
    return (two_cos, source.astype(jnp.float32))


def plane_inverse(spectral, table_y, table_z):
    physical = jnp.einsum("ly,xlm->xym", table_y, spectral, precision=precise)
    return jnp.einsum("mz,xym->xyz", table_z, physical, precision=precise)


def coupling_terms(own_strips, other_strips):
    weights = jnp.transpose(jnp.asarray(stencil_rows, dtype=jnp.float32)) / 180.0
    low_terms = jnp.einsum(
        "ij,...jw->...iw", weights[3:6, 0:3], other_strips[..., 0, :, :, :], precision=precise
    ) + jnp.einsum(
        "ij,...jw->...iw", weights[3:6, 3:6], own_strips[..., 0, :, :, :], precision=precise
    )
    high_terms = jnp.einsum(
        "ij,...jw->...iw", weights[0:3, 0:3], own_strips[..., 1, :, :, :], precision=precise
    ) + jnp.einsum(
        "ij,...jw->...iw", weights[0:3, 3:6], other_strips[..., 1, :, :, :], precision=precise
    )
    return jnp.stack([low_terms, high_terms], axis=-4)


def to_segments(strip_rows, pieces):
    x_cells, row_count, z_cells = strip_rows.shape
    layered = strip_rows.reshape(x_cells, row_count, pieces, z_cells // pieces)
    return jnp.transpose(layered, (2, 1, 0, 3)).reshape(
        pieces, row_count, x_cells * (z_cells // pieces)
    )


def from_segments(values, x_cells):
    pieces, row_count, flat_width = values.shape
    layered = values.reshape(pieces, row_count, x_cells, flat_width // x_cells)
    return jnp.transpose(layered, (2, 1, 0, 3)).reshape(
        x_cells, row_count, pieces * (flat_width // x_cells)
    )


def local(adj_next, adj_later, box_sizes, holder, partner):
    part_count = holder.shape[0]
    seg_count = partner.shape[2]
    item_count = 2 * seg_count
    my_group = lax.axis_index("grp")
    my_column = lax.axis_index("sub")
    sub_count = lax.axis_size("sub")
    x_local = adj_next.shape[1]
    y_cells = adj_next.shape[2]
    z_cells = adj_next.shape[3]
    x_total = x_local * sub_count
    y_local = y_cells // sub_count
    seg_cells = z_cells // seg_count
    strip_width = x_local * seg_cells
    part_ids = jnp.arange(part_count, dtype=jnp.int32)
    my_part = jnp.sum(jnp.where(holder == my_group, part_ids, 0))
    len_x = box_sizes[my_part, 0]
    len_y = box_sizes[my_part, 1]
    table_x = cosine_table(x_total, len_x)
    table_y = cosine_table(y_cells, len_y)
    table_z = cosine_table(z_cells, jnp.int32(z_cells))
    face_table = jnp.concatenate(
        [table_y[:, 0:3], lax.dynamic_slice_in_dim(table_y, len_y - 3, 3, 1)], axis=1
    )
    two_cos, source = update_factors(len_x, len_y, my_column * y_local, y_local, x_total, z_cells)
    x_global = my_column * x_local + jnp.arange(x_local, dtype=jnp.int32)
    y_index = jnp.arange(y_cells, dtype=jnp.int32)
    inside = ((x_global[:, None, None] < len_x) & (y_index[None, :, None] < len_y)).astype(
        jnp.float32
    )
    link_ids = partner[my_part].reshape(item_count)
    is_wall = link_ids < 0
    safe_links = jnp.maximum(link_ids, 0)
    peer_part = safe_links // seg_count
    peer_seg = safe_links % seg_count
    peer_group = holder[peer_part]
    item_ids = jnp.arange(item_count, dtype=jnp.int32)
    peer_item = (1 - item_ids // seg_count) * seg_count + peer_seg
    x_limit = jnp.minimum(len_x, box_sizes[peer_part, 0])
    column_x = my_column * x_local + jnp.arange(strip_width, dtype=jnp.int32) // seg_cells
    joined = ((column_x[None, :] < x_limit[:, None]) & jnp.logical_not(is_wall)[:, None]).astype(
        jnp.float32
    )
    joined = joined.reshape(2, seg_count, 1, strip_width)

    def reverse_step(current, earlier):
        spectral = jnp.einsum("mz,xyz->xym", table_z, current[0], precision=precise)
        spectral = jnp.einsum("ly,xym->xlm", table_y, spectral, precision=precise)
        spectral = lax.all_to_all(spectral, "sub", split_axis=1, concat_axis=0, tiled=True)
        spectral = jnp.einsum("kx,xlm->klm", table_x, spectral, precision=precise)
        wave_part = jnp.einsum("kx,klm->xlm", table_x, two_cos * spectral, precision=precise)
        force_part = jnp.einsum("kx,klm->xlm", table_x, source * spectral, precision=precise)
        wave_part, force_part = (
            lax.all_to_all(wave_part, "sub", split_axis=0, concat_axis=1, tiled=True),
            lax.all_to_all(force_part, "sub", split_axis=0, concat_axis=1, tiled=True),
        )
        face_rows = plane_inverse(force_part, face_table, table_z)
        wave_part = plane_inverse(wave_part, table_y, table_z)
        low_rows = face_rows[:, 0:3, :]
        high_rows = face_rows[:, 3:6, :]
        own_strips = jnp.concatenate(
            [to_segments(low_rows, seg_count), to_segments(high_rows, seg_count)], axis=0
        )
        everyone = lax.all_gather(own_strips[None], "grp", axis=0, tiled=True)
        everyone = everyone.reshape(part_count * item_count, 3, strip_width)
        other_strips = everyone[peer_group * item_count + peer_item]
        coupled = coupling_terms(
            own_strips.reshape(2, seg_count, 3, strip_width),
            other_strips.reshape(2, seg_count, 3, strip_width),
        )
        coupled = coupled * joined
        result = wave_part - inside * earlier[0]
        result = result.at[:, 0:3, :].add(from_segments(coupled[0], x_local))
        window = lax.dynamic_slice_in_dim(result, len_y - 3, 3, 1)
        result = lax.dynamic_update_slice_in_dim(
            result, window + from_segments(coupled[1], x_local), len_y - 3, 1
        )
        return result[None]

    adj_now = reverse_step(adj_next, adj_later)
    adj_earlier = reverse_step(adj_now, adj_next)
    return (adj_now, adj_earlier)


def solution(mesh):
    return jax.shard_map(
        local,
        mesh=mesh,
        in_specs=(P("grp", "sub", None, None), P("grp", "sub", None, None), P(), P(), P()),
        out_specs=(P("grp", "sub", None, None), P("grp", "sub", None, None)),
        check_vma=False,
    )
```

profile of v0, /device:TPU:1, one launch (start us, length us, event | category | flops | bytes accessed | tf_op | source)
XLA Modules:
  0.0 377.0 jit_solution(16978702654708273522)
XLA Ops:
  13.1 3.8 %fusion.15 = f32[128,32,128]{2,0,1:T(8,128)S(1)} fusion(f32[1,32,128,128]{3,2,1,0:T(8,128)} %param.11, f32[128]{0:T(128)S(1)} %get-tuple-element.45, f32[128]{0:T(128)S(1)} %get-tuple-element.46, f32[128]{0:T(128)S(1)} %get-tuple-element.47, pred[128]{0:T(512)(128)(4,1)S(1)} %iota_compare_fusion.1), kind=kOutput, calls=%fused_computation.27 | convolution fusion | flops 805388288 | bytes 4195968 | tf_op jit(solution)/shard_map/mz,xyz->xym/dot_general | solution.py:126
  20.9 5.0 %all-to-all-start = ((f32[32,128,128]{2,0,1:T(8,128)}), f32[32,128,128]{2,0,1:T(8,128)S(1)}, u32[]{:S(2)}, u32[]{:S(2)}) async-start(f32[32,128,128]{2,0,1:T(8,128)} %copy.159), calls=%async_computation | async-start | bytes 4194304 | tf_op jit(solution)/shard_map/all_to_all | solution.py:128
  27.2 23.2 %all-to-all-done = f32[32,128,128]{2,0,1:T(8,128)S(1)} async-done(((f32[32,128,128]{2,0,1:T(8,128)}), f32[32,128,128]{2,0,1:T(8,128)S(1)}, u32[]{:S(2)}, u32[]{:S(2)}) %all-to-all-start) | async-done | bytes 2097184 | tf_op jit(solution)/shard_map/all_to_all | solution.py:128
  52.8 5.3 %fusion.22 = f32[128,32,128]{2,0,1:T(8,128)S(1)} fusion(f32[128,32,128]{2,0,1:T(8,128)S(1)} %fusion.91, f32[128]{0:T(128)S(1)} %multiply_multiply_fusion.5, f32[128,32]{0,1:T(8,128)S(1)} %broadcast_add_fusion, f32[]{:T(128)S(6)} %convert_element_type.81, f32[128]{0:T(128)S(1)} %get-tuple-element.46, f32[128]{0:T(128)S(1)} %get-tuple-element.47, ...), kind=kOutput, calls=%fused_computation.34 | convolution fusion | flops 825311232 | bytes 4212868 | tf_op jit(solution)/shard_map/kx,klm->xlm/dot_general | solution.py:131
  60.7 4.4 %all-to-all-start.2 = ((f32[128,32,128]{2,1,0:T(8,128)}), f32[128,32,128]{2,1,0:T(8,128)}, u32[]{:S(2)}, u32[]{:S(2)}) async-start(f32[128,32,128]{2,1,0:T(8,128)} %copy.169), calls=%async_computation.2 | async-start | bytes 4194304 | tf_op jit(solution)/shard_map/all_to_all | solution.py:134
  67.1 21.8 %all-to-all-done.2 = f32[128,32,128]{2,1,0:T(8,128)} async-done(((f32[128,32,128]{2,1,0:T(8,128)}), f32[128,32,128]{2,1,0:T(8,128)}, u32[]{:S(2)}, u32[]{:S(2)}) %all-to-all-start.2) | async-done | bytes 2097184 | tf_op jit(solution)/shard_map/all_to_all | solution.py:134
  93.7 10.1 %fusion.30 = f32[128,32,128]{2,0,1:T(8,128)S(1)} fusion(f32[128,32,128]{2,0,1:T(8,128)S(1)} %fusion.91, f32[128]{0:T(128)S(1)} %multiply_multiply_fusion.5, f32[128,32]{0,1:T(8,128)S(1)} %broadcast_add_fusion, f32[]{:T(128)S(6)} %convert_element_type.81, f32[128]{0:T(128)S(1)} %get-tuple-element.46, f32[128]{0:T(128)S(1)} %get-tuple-element.47, ...), kind=kOutput, calls=%fused_computation.47 | convolution fusion | flops 807485440 | bytes 4212868 | tf_op jit(solution)/shard_map/kx,klm->xlm/dot_general | solution.py:130
  106.4 3.7 all-to-all-start.1
  113.7 19.2 %all-to-all-done.1 = f32[128,32,128]{2,1,0:T(8,128)S(1)} async-done(((f32[128,32,128]{2,1,0:T(8,128)}), f32[128,32,128]{2,1,0:T(8,128)S(1)}, u32[]{:S(2)}, u32[]{:S(2)}) %all-to-all-start.1) | async-done | bytes 2097184 | tf_op jit(solution)/shard_map/all_to_all | solution.py:133
  134.1 3.6 fusion.71
  137.7 4.2 %fusion.10 = f32[32,128,128]{2,1,0:T(8,128)S(1)} fusion(f32[1,32,128,128]{3,2,1,0:T(8,128)S(1)} %copy-done.5, f32[32,128,128]{2,1,0:T(8,128)S(1)} %fusion.71, f32[32,128]{1,0:T(8,128)S(1)} %and_convert_fusion.1, f32[128]{0:T(128)S(1)} %get-tuple-element.45, f32[128]{0:T(128)S(1)} %get-tuple-element.46, f32[128]{0:T(128)S(1)} %get-tuple-element.47, ...), kind=kOutput, calls=%fused_computation.21 | convolution fusion | flops 806436864 | bytes 6309504 | tf_op jit(solution)/shard_map/mz,xym->xyz/dot_general | solution.py:46
  141.9 38.0 %all-gather.5.cloned.1.call-done = f32[512,3,1024]{2,0,1:T(8,128)} async-done(((f32[8,3,1024]{2,0,1:T(8,128)}), f32[512,3,1024]{2,0,1:T(8,128)}) %all-gather.5.cloned.1.call-update) | async-done | bytes 6291472 | tf_op jit(solution)/shard_map/all_gather | solution.py:143
  179.9 10.5 %copy.175 = f32[512,3,1024]{2,1,0:T(4,128)} copy(f32[512,3,1024]{2,0,1:T(8,128)} %all-gather.5.cloned.1.call-done) | data formatting | bytes 12582912 | tf_op jit(solution)/shard_map/all_gather | solution.py:143
  190.4 4.0 %gather_fusion.1 = f32[8,3,1024]{2,1,0:T(4,128)S(1)} fusion(f32[512,3,1024]{2,1,0:T(4,128)} %copy.175, s32[1024]{0:T(1024)S(1)} %pad_clamp_fusion), kind=kCustom, calls=%fused_computation.1 | custom fusion | bytes 196640 | tf_op jit(solution)/shard_map/gather | solution.py:145
  204.7 29.8 %all_to_all.108 = f32[32,128,128]{2,0,1:T(8,128)S(1)} all-to-all(f32[32,128,128]{2,0,1:T(8,128)S(1)} %copy.187), channel_id=1, replica_groups=mesh['grp'=64,'sub'=4] {'sub'}, dimensions={1} | all-to-all | bytes 4194304 | tf_op jit(solution)/shard_map/all_to_all | solution.py:128
  237.0 5.3 %fusion.18 = f32[128,32,128]{2,0,1:T(8,128)S(1)} fusion(f32[128,32,128]{2,0,1:T(8,128)S(1)} %fusion.89, f32[128]{0:T(128)S(1)} %multiply_multiply_fusion.5, f32[128,32]{0,1:T(8,128)S(1)} %broadcast_add_fusion, f32[]{:T(128)S(6)} %convert_element_type.81, f32[128]{0:T(128)S(1)} %get-tuple-element.46, f32[128]{0:T(128)S(1)} %get-tuple-element.47, ...), kind=kOutput, calls=%fused_computation.30 | convolution fusion | flops 825311232 | bytes 4212868 | tf_op jit(solution)/shard_map/kx,klm->xlm/dot_general | solution.py:131
  243.6 27.2 %all_to_all.109 = f32[128,32,128]{2,1,0:T(8,128)S(1)} all-to-all(f32[128,32,128]{2,1,0:T(8,128)S(1)} %copy.197), channel_id=1, replica_groups=mesh['grp'=64,'sub'=4] {'sub'}, dimensions={0} | all-to-all | bytes 4194304 | tf_op jit(solution)/shard_map/all_to_all | solution.py:134
  274.1 9.9 %fusion.20 = f32[128,32,128]{2,0,1:T(8,128)S(1)} fusion(f32[128,32,128]{2,0,1:T(8,128)S(1)} %fusion.89, f32[128]{0:T(128)S(1)} %multiply_multiply_fusion.5, f32[128,32]{0,1:T(8,128)S(1)} %broadcast_add_fusion, f32[]{:T(128)S(6)} %convert_element_type.81, f32[128]{0:T(128)S(1)} %get-tuple-element.46, f32[128]{0:T(128)S(1)} %get-tuple-element.47, ...), kind=kOutput, calls=%fused_computation.32 | convolution fusion | flops 807485440 | bytes 4212868 | tf_op jit(solution)/shard_map/kx,klm->xlm/dot_general | solution.py:130
  285.2 26.3 %all_to_all.110 = f32[128,32,128]{2,1,0:T(8,128)S(1)} all-to-all(f32[128,32,128]{2,1,0:T(8,128)S(1)} %copy.191), channel_id=1, replica_groups=mesh['grp'=64,'sub'=4] {'sub'}, dimensions={0} | all-to-all | bytes 4194304 | tf_op jit(solution)/shard_map/all_to_all | solution.py:133
  312.3 3.6 fusion.68
  315.9 4.3 %fusion.17 = f32[32,128,128]{2,1,0:T(8,128)S(1)} fusion(f32[1,32,128,128]{3,2,1,0:T(8,128)S(1)} %copy-done.3, f32[32,128,128]{2,1,0:T(8,128)S(1)} %fusion.68, f32[32,128]{1,0:T(8,128)S(1)} %and_convert_fusion.1, f32[128]{0:T(128)S(1)} %get-tuple-element.45, f32[128]{0:T(128)S(1)} %get-tuple-element.46, f32[128]{0:T(128)S(1)} %get-tuple-element.47, ...), kind=kOutput, calls=%fused_computation.29 | convolution fusion | flops 806436864 | bytes 6309504 | tf_op jit(solution)/shard_map/mz,xym->xyz/dot_general | solution.py:46
  320.2 31.8 %all-gather.7.cloned.1.call-done = f32[512,3,1024]{2,0,1:T(8,128)} async-done(((f32[8,3,1024]{2,0,1:T(8,128)}), f32[512,3,1024]{2,0,1:T(8,128)}) %all-gather.7.cloned.1.call-update) | async-done | bytes 6291472 | tf_op jit(solution)/shard_map/all_gather | solution.py:143
  352.0 10.5 %copy.203 = f32[512,3,1024]{2,1,0:T(4,128)} copy(f32[512,3,1024]{2,0,1:T(8,128)} %all-gather.7.cloned.1.call-done) | data formatting | bytes 12582912 | tf_op jit(solution)/shard_map/all_gather | solution.py:143
  362.5 4.0 %gather_fusion.3 = f32[8,3,1024]{2,1,0:T(4,128)S(1)} fusion(f32[512,3,1024]{2,1,0:T(4,128)} %copy.203, s32[1024]{0:T(1024)S(1)} %pad_clamp_fusion), kind=kCustom, calls=%fused_computation.3 | custom fusion | bytes 196640 | tf_op jit(solution)/shard_map/gather | solution.py:145
  (129 shorter events, 47.9 us)
Async XLA Ops:
  20.9 29.5 %all-to-all-start = ((f32[32,128,128]{2,0,1:T(8,128)}), f32[32,128,128]{2,0,1:T(8,128)S(1)}, u32[]{:S(2)}, u32[]{:S(2)}) async-start(f32[32,128,128]{2,0,1:T(8,128)} %copy.159), calls=%async_computation | async-start | bytes 4194304 | tf_op jit(solution)/shard_map/all_to_all | solution.py:128
  60.7 28.1 %all-to-all-start.2 = ((f32[128,32,128]{2,1,0:T(8,128)}), f32[128,32,128]{2,1,0:T(8,128)}, u32[]{:S(2)}, u32[]{:S(2)}) async-start(f32[128,32,128]{2,1,0:T(8,128)} %copy.169), calls=%async_computation.2 | async-start | bytes 4194304 | tf_op jit(solution)/shard_map/all_to_all | solution.py:134
  65.2 114.8 %all-gather.5.cloned.1.call-start = ((), (), s32[]{:S(2)}) async-start(), calls=%async_computation.6 | async-start | bytes 6389760 | tf_op jit(solution)/shard_map/all_gather | solution.py:143
  106.4 3.8 %copy-start.6 = (s32[64,2,4]{0,2,1:T(4,128)S(1)}, s32[64,2,4]{0,2,1:T(4,128)}, u32[]{:S(2)}) copy-start(s32[64,2,4]{0,2,1:T(4,128)} %param.15) | copy-start | bytes 6148
  106.4 4.5 %copy-start = (s32[64]{0:T(128)S(1)}, s32[64]{0:T(128)}, u32[]{:S(2)}) copy-start(s32[64]{0:T(128)} %param.14) | copy-start | bytes 772
  106.4 5.2 %copy-start.1 = (s32[64,2]{0,1:T(2,128)S(1)}, s32[64,2]{0,1:T(2,128)}, u32[]{:S(2)}) copy-start(s32[64,2]{0,1:T(2,128)} %param.13) | copy-start | bytes 1540
  106.4 26.5 %all-to-all-start.1 = ((f32[128,32,128]{2,1,0:T(8,128)}), f32[128,32,128]{2,1,0:T(8,128)S(1)}, u32[]{:S(2)}, u32[]{:S(2)}) async-start(f32[128,32,128]{2,1,0:T(8,128)} %copy.163), calls=%async_computation.1 | async-start | bytes 4194304 | tf_op jit(solution)/shard_map/all_to_all | solution.py:133
  110.1 241.8 %all-gather.7.cloned.1.call-start = ((), (), s32[]{:S(2)}) async-start(), calls=%async_computation.7 | async-start | bytes 6389760 | tf_op jit(solution)/shard_map/all_gather | solution.py:143
  132.8 0.7 copy-start.10
  132.8 0.9 copy-start.9
  134.1 3.6 copy-start.5
  141.9 52.6 %copy-start.8 = (f32[3,3,1]{1,0,2:T(4,128)S(1)}, f32[3,3,1]{1,0,2:T(4,128)}, u32[]{:S(2)}) copy-start(f32[3,3,1]{1,0,2:T(4,128)} %constant.231) | copy-start | bytes 112
  141.9 52.8 %copy-start.7 = (f32[3,3,1]{1,0,2:T(4,128)S(1)}, f32[3,3,1]{1,0,2:T(4,128)}, u32[]{:S(2)}) copy-start(f32[3,3,1]{1,0,2:T(4,128)} %constant.228) | copy-start | bytes 112
  196.6 2.4 copy-start.2
  312.3 3.6 copy-start.3
  368.6 1.3 copy-start.4
Sparse Core Ops, SparseCore 0:
  93.8 86.0 all-gather.4
  274.2 77.6 all-gather.6
where the time goes:
time: 382 us; the launch traced here: 377 us
  waiting for transfers between devices  134 us (35%)
  blocking collectives  83.4 us (22%)
  matrix products  67.9 us (18%)
  local copies, waits for them, and re-layouts  52.6 us (14%)
  between operations  19.5 us (5%)
  starting transfers between devices  13.5 us (4%)
  other arithmetic  6.25 us (2%)
    all_gather x2, waiting for transfers between devices, reverse_step(): everyone = lax.all_gather(own_strips[None], 'grp', axis=0, tiled=True)  69.8 us
    all_to_all x1, blocking collectives, reverse_step(): lax.all_to_all(spectral, 'sub', split_axis=1, concat_axis=0, tiled=True)  29.8 us
    all_to_all x1, blocking collectives, reverse_step(): lax.all_to_all(force_part, 'sub', split_axis=0, concat_axis=1, tiled=True)  27.2 us
    all_to_all x1, blocking collectives, reverse_step(): lax.all_to_all(wave_part, 'sub', split_axis=0, concat_axis=1, tiled=True)  26.3 us
    all_to_all x1, waiting for transfers between devices, reverse_step(): lax.all_to_all(spectral, 'sub', split_axis=1, concat_axis=0, tiled=True)  23.2 us
    all_to_all x1, waiting for transfers between devices, reverse_step(): lax.all_to_all(force_part, 'sub', split_axis=0, concat_axis=1, tiled=True)  21.8 us
    all_gather x2, local copies, waits for them, and re-layouts, reverse_step(): everyone = lax.all_gather(own_strips[None], 'grp', axis=0, tiled=True)  21 us
    dot_general x2, matrix products, reverse_step(): jnp.einsum('kx,klm->xlm', table_x, two_cos * spectral, precision=precise)  20 us
  transfers between devices with their start and end apart: 5, of which 5 were waited for; matrix products, arithmetic and copies ran while one was open for 12% of the time, Pallas kernels for 0%

commit v1 on v0

--- a/solution.py
+++ b/solution.py
@@ -140,7 +140,10 @@
         own_strips = jnp.concatenate(
             [to_segments(low_rows, seg_count), to_segments(high_rows, seg_count)], axis=0
         )
-        everyone = lax.all_gather(own_strips[None], "grp", axis=0, tiled=True)
+        everyone = jnp.concatenate(
+            lax.all_to_all(jnp.stack([own_strips[None]] * lax.axis_size("grp")), "grp", 0, 0),
+            axis=0,
+        )
         everyone = everyone.reshape(part_count * item_count, 3, strip_width)
         other_strips = everyone[peer_group * item_count + peer_item]
         coupled = coupling_terms(

time: 382 us -> 576 us (1.51)
  waiting for transfers between devices: 134 us -> 342 us
  blocking collectives: 83.4 us -> 29.4 us
  starting transfers between devices: 13.5 us -> 47.2 us
  local copies, waits for them, and re-layouts: 52.6 us -> 70.6 us
  between operations: 19.5 us -> 6.06 us
    all_to_all x0 -> x2, waiting for transfers between devices: none -> 260 us  [reverse_step(): lax.all_to_all(jnp.stack([own_strips[None]] * lax.axis_size('grp')), 'grp...]
    all_gather x2 -> x0, waiting for transfers between devices: 69.8 us -> none  [reverse_step(): everyone = lax.all_gather(own_strips[None], 'grp', axis=0, tiled=True)]
    all_to_all x2 -> x0, blocking collectives: 53.5 us -> none  [the longest x1 27.2 us: reverse_step(): lax.all_to_all(force_part, 'sub', split_axis=0, concat_axis=1, tiled=True)]
    all_to_all x0 -> x2, starting transfers between devices: none -> 27.2 us  [reverse_step(): lax.all_to_all(jnp.stack([own_strips[None]] * lax.axis_size('grp')), 'grp...]
    another operation x4 -> x8, local copies, waits for them, and re-layouts: 0.58 us -> 23 us  [the longest x2 15.6 us: reverse_step(): everyone = everyone.reshape(part_count * item_count, 3, strip_width)]
    all_gather x2 -> x0, local copies, waits for them, and re-layouts: 21 us -> none  [reverse_step(): everyone = lax.all_gather(own_strips[None], 'grp', axis=0, tiled=True)]
    all_to_all x1 -> x2, waiting for transfers between devices: 19.2 us -> 37.6 us  [reverse_step(): lax.all_to_all(wave_part, 'sub', split_axis=0, concat_axis=1, tiled=True)]
    all_to_all x0 -> x2, local copies, waits for them, and re-layouts: none -> 7.11 us  [reverse_step(): lax.all_to_all(jnp.stack([own_strips[None]] * lax.axis_size('grp')), 'grp...]
  transfers between devices with their start and end apart: 5 -> 7, of which waited for: 5 -> 7; matrix products, arithmetic and copies ran while one was open for 12% -> 10% of each run, Pallas kernels for 0% -> 0%
where the time goes in v1:
time: 576 us; the launch traced here: 571 us
  waiting for transfers between devices  342 us (59%)
  local copies, waits for them, and re-layouts  70.6 us (12%)
  matrix products  70.4 us (12%)
  starting transfers between devices  47.2 us (8%)
  blocking collectives  29.4 us (5%)
  between operations  6.06 us (1%)
    all_to_all x2, waiting for transfers between devices, reverse_step(): lax.all_to_all(jnp.stack([own_strips[None]] * lax.axis_size('grp')), 'grp...  260 us
    all_to_all x2, waiting for transfers between devices, reverse_step(): lax.all_to_all(wave_part, 'sub', split_axis=0, concat_axis=1, tiled=True)  37.6 us
    all_to_all x1, blocking collectives, reverse_step(): lax.all_to_all(spectral, 'sub', split_axis=1, concat_axis=0, tiled=True)  29.4 us
    all_to_all x2, starting transfers between devices, reverse_step(): lax.all_to_all(jnp.stack([own_strips[None]] * lax.axis_size('grp')), 'grp...  27.2 us
    all_to_all x1, waiting for transfers between devices, reverse_step(): lax.all_to_all(spectral, 'sub', split_axis=1, concat_axis=0, tiled=True)  23.1 us
    dot_general x2, matrix products, reverse_step(): jnp.einsum('kx,klm->xlm', table_x, two_cos * spectral, precision=precise)  22.6 us
    all_to_all x2, waiting for transfers between devices, reverse_step(): lax.all_to_all(force_part, 'sub', split_axis=0, concat_axis=1, tiled=True)  21.6 us
    another operation x2, local copies, waits for them, and re-layouts, reverse_step(): everyone = everyone.reshape(part_count * item_count, 3, strip_width)  15.6 us
  transfers between devices with their start and end apart: 7, of which 7 were waited for; matrix products, arithmetic and copies ran while one was open for 10% of the time, Pallas kernels for 0%

profile of v1, /device:TPU:1, one launch (start us, length us, event | category | flops | bytes accessed | tf_op | source)
XLA Modules:
  0.0 571.0 jit_solution(10243723752337649956)
XLA Ops:
  6.4 3.8 fusion.15
  14.3 5.0 all-to-all-start
  20.7 23.1 %all-to-all-done = f32[32,128,128]{2,0,1:T(8,128)S(1)} async-done(((f32[32,128,128]{2,0,1:T(8,128)}), f32[32,128,128]{2,0,1:T(8,128)S(1)}, u32[]{:S(2)}, u32[]{:S(2)}) %all-to-all-start) | async-done | bytes 2097184 | tf_op jit(solution)/shard_map/all_to_all | solution.py:128
  47.5 5.3 fusion.22
  55.4 4.0 all-to-all-start.2
  59.4 11.3 %fusion.30 = f32[128,32,128]{2,0,1:T(8,128)S(1)} fusion(f32[128,32,128]{2,0,1:T(8,128)} %copy-done.7, f32[128]{0:T(128)S(1)} %multiply_multiply_fusion.5, f32[128,32]{0,1:T(8,128)S(1)} %broadcast_add_fusion, f32[]{:T(128)S(6)} %convert_element_type.81, f32[128]{0:T(128)S(1)} %get-tuple-element.46, f32[128]{0:T(128)S(1)} %get-tuple-element.47, ...), kind=kOutput, calls=%fused_computation.49 | convolution fusion | flops 807485440 | bytes 4212868 | tf_op jit(solution)/shard_map/kx,klm->xlm/dot_general | solution.py:130
  73.3 9.7 %all-to-all-done.2 = f32[128,32,128]{2,1,0:T(8,128)S(1)} async-done(((f32[128,32,128]{2,1,0:T(8,128)}), f32[128,32,128]{2,1,0:T(8,128)S(1)}, u32[]{:S(2)}, u32[]{:S(2)}) %all-to-all-start.2) | async-done | bytes 2097184 | tf_op jit(solution)/shard_map/all_to_all | solution.py:134
  93.6 17.1 %all-to-all-done.1 = f32[128,32,128]{2,1,0:T(8,128)S(1)} async-done(((f32[128,32,128]{2,1,0:T(8,128)}), f32[128,32,128]{2,1,0:T(8,128)S(1)}, u32[]{:S(2)}, u32[]{:S(2)}) %all-to-all-start.1) | async-done | bytes 2097184 | tf_op jit(solution)/shard_map/all_to_all | solution.py:133
  114.1 18.6 %all-to-all-start.3 = ((f32[64,1,8,3,1024]{4,2,3,1,0:T(8,128)}), f32[64,1,8,3,1024]{4,2,3,1,0:T(8,128)}, u32[]{:S(2)}, u32[]{:S(2)}) async-start(f32[64,1,8,3,1024]{4,2,3,1,0:T(8,128)} %stack.24), calls=%async_computation.3 | async-start | bytes 12582912 | tf_op jit(solution)/shard_map/all_to_all | solution.py:144
  141.2 4.2 fusion.10
  145.4 127.9 %all-to-all-done.3 = f32[64,1,8,3,1024]{4,2,3,1,0:T(8,128)} async-done(((f32[64,1,8,3,1024]{4,2,3,1,0:T(8,128)}), f32[64,1,8,3,1024]{4,2,3,1,0:T(8,128)}, u32[]{:S(2)}, u32[]{:S(2)}) %all-to-all-start.3) | async-done | bytes 6291488 | tf_op jit(solution)/shard_map/all_to_all | solution.py:144
  276.9 7.8 %copy.180 = f32[512,3,1024]{2,1,0:T(4,128)} copy(f32[512,3,1024]{2,0,1:T(8,128)S(1)} %bitcast.205) | data formatting | bytes 12582912 | tf_op jit(solution)/shard_map/reshape;reshape | solution.py:147
  284.7 4.0 gather_fusion.1
  299.0 29.4 %all_to_all.118 = f32[32,128,128]{2,0,1:T(8,128)S(1)} all-to-all(f32[32,128,128]{2,0,1:T(8,128)S(1)} %copy.192), channel_id=1, replica_groups=mesh['grp'=64,'sub'=4] {'sub'}, dimensions={1} | all-to-all | bytes 4194304 | tf_op jit(solution)/shard_map/all_to_all | solution.py:128
  332.2 5.3 fusion.18
  340.1 3.8 all-to-all-start.6
  343.9 11.3 %fusion.20 = f32[128,32,128]{2,0,1:T(8,128)S(1)} fusion(f32[128,32,128]{2,0,1:T(8,128)} %copy-done.6, f32[128]{0:T(128)S(1)} %multiply_multiply_fusion.5, f32[128,32]{0,1:T(8,128)S(1)} %broadcast_add_fusion, f32[]{:T(128)S(6)} %convert_element_type.81, f32[128]{0:T(128)S(1)} %get-tuple-element.46, f32[128]{0:T(128)S(1)} %get-tuple-element.47, ...), kind=kOutput, calls=%fused_computation.34 | convolution fusion | flops 807485440 | bytes 4212868 | tf_op jit(solution)/shard_map/kx,klm->xlm/dot_general | solution.py:130
  357.7 11.8 %all-to-all-done.6 = f32[128,32,128]{2,1,0:T(8,128)S(1)} async-done(((f32[128,32,128]{2,1,0:T(8,128)}), f32[128,32,128]{2,1,0:T(8,128)S(1)}, u32[]{:S(2)}, u32[]{:S(2)}) %all-to-all-start.6) | async-done | bytes 2097184 | tf_op jit(solution)/shard_map/all_to_all | solution.py:134
  378.7 20.6 %all-to-all-done.5 = f32[128,32,128]{2,1,0:T(8,128)S(1)} async-done(((f32[128,32,128]{2,1,0:T(8,128)}), f32[128,32,128]{2,1,0:T(8,128)S(1)}, u32[]{:S(2)}, u32[]{:S(2)}) %all-to-all-start.5) | async-done | bytes 2097184 | tf_op jit(solution)/shard_map/all_to_all | solution.py:133
  402.7 8.6 %all-to-all-start.7 = ((f32[64,1,8,3,1024]{4,2,3,1,0:T(8,128)}), f32[64,1,8,3,1024]{4,2,3,1,0:T(8,128)}, u32[]{:S(2)}, u32[]{:S(2)}) async-start(f32[64,1,8,3,1024]{4,2,3,1,0:T(8,128)} %stack.28), calls=%async_computation.7 | async-start | bytes 12582912 | tf_op jit(solution)/shard_map/all_to_all | solution.py:144
  415.7 4.2 fusion.17
  419.9 132.0 %all-to-all-done.7 = f32[64,1,8,3,1024]{4,2,3,1,0:T(8,128)} async-done(((f32[64,1,8,3,1024]{4,2,3,1,0:T(8,128)}), f32[64,1,8,3,1024]{4,2,3,1,0:T(8,128)}, u32[]{:S(2)}, u32[]{:S(2)}) %all-to-all-start.7) | async-done | bytes 6291488 | tf_op jit(solution)/shard_map/all_to_all | solution.py:144
  555.5 7.8 %copy.209 = f32[512,3,1024]{2,1,0:T(4,128)} copy(f32[512,3,1024]{2,0,1:T(8,128)S(1)} %bitcast.206) | data formatting | bytes 12582912 | tf_op jit(solution)/shard_map/reshape;reshape | solution.py:147
  563.3 4.0 gather_fusion.3
  (141 shorter events, 84.2 us)
Async XLA Ops:
  14.3 29.5 %all-to-all-start = ((f32[32,128,128]{2,0,1:T(8,128)}), f32[32,128,128]{2,0,1:T(8,128)S(1)}, u32[]{:S(2)}, u32[]{:S(2)}) async-start(f32[32,128,128]{2,0,1:T(8,128)} %copy.163), calls=%async_computation | async-start | bytes 4194304 | tf_op jit(solution)/shard_map/all_to_all | solution.py:128
  46.2 1.3 copy-start.7
  55.4 27.6 %all-to-all-start.2 = ((f32[128,32,128]{2,1,0:T(8,128)}), f32[128,32,128]{2,1,0:T(8,128)S(1)}, u32[]{:S(2)}, u32[]{:S(2)}) async-start(f32[128,32,128]{2,1,0:T(8,128)} %copy.173), calls=%async_computation.2 | async-start | bytes 4194304 | tf_op jit(solution)/shard_map/all_to_all | solution.py:134
  83.0 1.3 copy-start.4
  84.3 26.4 %all-to-all-start.1 = ((f32[128,32,128]{2,1,0:T(8,128)}), f32[128,32,128]{2,1,0:T(8,128)S(1)}, u32[]{:S(2)}, u32[]{:S(2)}) async-start(f32[128,32,128]{2,1,0:T(8,128)} %copy.167), calls=%async_computation.1 | async-start | bytes 4194304 | tf_op jit(solution)/shard_map/all_to_all | solution.py:133
  114.1 18.6 %copy-start.10 = (s32[64,2,4]{0,2,1:T(4,128)S(1)}, s32[64,2,4]{0,2,1:T(4,128)}, u32[]{:S(2)}) copy-start(s32[64,2,4]{0,2,1:T(4,128)} %param.15) | copy-start | bytes 6148
  114.1 19.4 %copy-start = (s32[64]{0:T(128)S(1)}, s32[64]{0:T(128)}, u32[]{:S(2)}) copy-start(s32[64]{0:T(128)} %param.14) | copy-start | bytes 772
  114.1 20.0 %copy-start.1 = (s32[64,2]{0,1:T(2,128)S(1)}, s32[64,2]{0,1:T(2,128)}, u32[]{:S(2)}) copy-start(s32[64,2]{0,1:T(2,128)} %param.13) | copy-start | bytes 1540
  114.1 159.3 %all-to-all-start.3 = ((f32[64,1,8,3,1024]{4,2,3,1,0:T(8,128)}), f32[64,1,8,3,1024]{4,2,3,1,0:T(8,128)}, u32[]{:S(2)}, u32[]{:S(2)}) async-start(f32[64,1,8,3,1024]{4,2,3,1,0:T(8,128)} %stack.24), calls=%async_computation.3 | async-start | bytes 12582912 | tf_op jit(solution)/shard_map/all_to_all | solution.py:144
  136.3 0.7 copy-start.14
  136.4 0.9 copy-start.13
  137.6 3.6 copy-start.9
  276.9 11.8 %copy-start.12 = (f32[3,3,1]{1,0,2:T(4,128)S(1)}, f32[3,3,1]{1,0,2:T(4,128)}, u32[]{:S(2)}) copy-start(f32[3,3,1]{1,0,2:T(4,128)} %constant.231) | copy-start | bytes 112
  276.9 12.1 %copy-start.11 = (f32[3,3,1]{1,0,2:T(4,128)S(1)}, f32[3,3,1]{1,0,2:T(4,128)}, u32[]{:S(2)}) copy-start(f32[3,3,1]{1,0,2:T(4,128)} %constant.228) | copy-start | bytes 112
  290.9 2.4 copy-start.2
  330.9 1.3 copy-start.6
  340.1 29.4 %all-to-all-start.6 = ((f32[128,32,128]{2,1,0:T(8,128)}), f32[128,32,128]{2,1,0:T(8,128)S(1)}, u32[]{:S(2)}, u32[]{:S(2)}) async-start(f32[128,32,128]{2,1,0:T(8,128)} %copy.202), calls=%async_computation.6 | async-start | bytes 4194304 | tf_op jit(solution)/shard_map/all_to_all | solution.py:134
  369.6 1.3 copy-start.5
  370.9 28.4 %all-to-all-start.5 = ((f32[128,32,128]{2,1,0:T(8,128)}), f32[128,32,128]{2,1,0:T(8,128)S(1)}, u32[]{:S(2)}, u32[]{:S(2)}) async-start(f32[128,32,128]{2,1,0:T(8,128)} %copy.196), calls=%async_computation.5 | async-start | bytes 4194304 | tf_op jit(solution)/shard_map/all_to_all | solution.py:133
  402.7 149.2 %all-to-all-start.7 = ((f32[64,1,8,3,1024]{4,2,3,1,0:T(8,128)}), f32[64,1,8,3,1024]{4,2,3,1,0:T(8,128)}, u32[]{:S(2)}, u32[]{:S(2)}) async-start(f32[64,1,8,3,1024]{4,2,3,1,0:T(8,128)} %stack.28), calls=%async_computation.7 | async-start | bytes 12582912 | tf_op jit(solution)/shard_map/all_to_all | solution.py:144
  412.0 3.6 copy-start.3
  569.4 1.3 copy-start.8
